TPU v7x, 32 devices: a whole 2x2x4 slice. The times are simulated.
32 devices in a mesh: aa: 8 (over z, x), ba: 4 (over y, core).
Axes of the slice: x: 2, y: 2, z: 4, core: 2. Of those that a mesh axis runs over, the one named last changes fastest.
Arguments:
- features_a: bfloat16 [16, 32, 256], P('aa', 'ba'), may hold values from -9 to 9
- features_b: bfloat16 [16, 128, 256], P('ba', 'aa'), may hold values from -9 to 9
- conv_in: float32 [8, 3, 3, 3, 3], replicated, may hold values from -0.625 to 0.625
- bias_in: float32 [8], replicated, may hold values from -1 to 1
- conv_out: float32 [8, 3, 3, 3, 3], replicated, may hold values from -0.25 to 0.25
Outputs:
- log_mutual: float32 [16, 32, 16, 128], P('aa', None, 'ba')
- warped: float32 [16, 32, 256], P('aa', 'ba')
All inputs are finite; a program needn't handle non-finite values.
Results may differ from a plain program's by a relative error of at most 0.0035.
Values may be sent and summed in bfloat16 or wider, within the bound.
No kernel may reach another device: no remote copies, remote signals or barrier semaphores. Data moves between devices by JAX's collectives and lax.ppermute only.
A program may use at most 64 MiB of HBM per device.

v0:
```python
import math
import jax
import jax.numpy as jnp
from jax import lax
from jax.sharding import PartitionSpec as P


def padded_2(cells, sides, width):
    for axis, dim in sides:
        count = lax.axis_size(axis)
        ends = count - 1
        head = lax.slice_in_dim(cells, 0, width, axis=dim)
        tail = lax.slice_in_dim(cells, cells.shape[dim] - width, cells.shape[dim], axis=dim)
        cells = jnp.concatenate(
            [
                lax.ppermute(tail, axis, [(i, (i + 1) % count) for i in range(ends)]),
                cells,
                lax.ppermute(head, axis, [((i + 1) % count, i) for i in range(ends)]),
            ],
            axis=dim,
        )
    return cells


def tap_offsets():
    return [
        (step_one, step_two, step_three, step_four)
        for step_one in range(3)
        for step_two in range(3)
        for step_three in range(3)
        for step_four in range(3)
    ]


def spread_taps(padded, kernel, bias_in):
    extent = [size_here - 2 for size_here in padded.shape]
    result = jnp.zeros([kernel.shape[0]] + extent, jnp.float32)
    for offsets in tap_offsets():
        window = padded[
            offsets[0] : offsets[0] + extent[0],
            offsets[1] : offsets[1] + extent[1],
            offsets[2] : offsets[2] + extent[2],
            offsets[3] : offsets[3] + extent[3],
        ]
        result = (
            result
            + kernel[:, offsets[0], offsets[1], offsets[2], offsets[3]].reshape(-1, 1, 1, 1, 1)
            * window[None]
        )
    return jax.nn.relu(result + bias_in.reshape(-1, 1, 1, 1, 1))


def reduce_taps(padded, kernel):
    extent = [size_here - 2 for size_here in padded.shape[1:]]
    result = jnp.zeros(extent, jnp.float32)
    for offsets in tap_offsets():
        window = padded[
            :,
            offsets[0] : offsets[0] + extent[0],
            offsets[1] : offsets[1] + extent[1],
            offsets[2] : offsets[2] + extent[2],
            offsets[3] : offsets[3] + extent[3],
        ]
        result = result + jnp.sum(
            kernel[:, offsets[0], offsets[1], offsets[2], offsets[3]].reshape(-1, 1, 1, 1, 1)
            * window,
            axis=0,
        )
    return result


def dual_norms(values):
    top_a = lax.pmax(jnp.max(values, axis=(0, 1)), "aa")
    top_b = lax.pmax(jnp.max(values, axis=(2, 3)), "ba")
    mass_a = lax.psum(jnp.sum(jnp.exp(values - top_a), axis=(0, 1)), "aa")
    mass_b = lax.psum(jnp.sum(jnp.exp(values - top_b[:, :, None, None]), axis=(2, 3)), "ba")
    norm_a = top_a + jnp.log(mass_a)
    norm_b = top_b + jnp.log(mass_b)
    return (norm_a, norm_b[:, :, None, None])


def local(features_a, features_b, conv_in, bias_in, conv_out):
    channels = features_a.shape[2]
    rows_a = lax.all_gather(features_a, "ba", axis=1, tiled=True)
    rows_b = lax.all_gather(features_b, "aa", axis=1, tiled=True)
    height_a = rows_a.shape[0]
    width_a = rows_a.shape[1]
    height_b = rows_b.shape[0]
    width_b = rows_b.shape[1]
    grid_a = height_a * lax.axis_size("aa")
    grid_b = height_b * lax.axis_size("ba")
    offset = math.log(grid_a * width_a * grid_b * width_b)
    scores = jnp.einsum(
        "xyc,uvc->xyuv", rows_a, rows_b, preferred_element_type=jnp.float32
    ) / math.sqrt(channels)
    norm_a, norm_b = dual_norms(scores)
    matched = jax.nn.softplus(2.0 * scores - norm_a - norm_b + offset)
    rim = padded_2(matched, (("aa", 0), ("ba", 2)), 1)
    hidden = spread_taps(jnp.pad(rim, ((0, 0), (1, 1), (0, 0), (1, 1))), conv_in, bias_in)
    rim_hidden = padded_2(hidden, (("aa", 1), ("ba", 3)), 1)
    filtered = reduce_taps(jnp.pad(rim_hidden, ((0, 0), (0, 0), (1, 1), (0, 0), (1, 1))), conv_out)
    refined = scores + jax.nn.relu(filtered)
    norm_a2, norm_b2 = dual_norms(refined)
    log_mutual = 2.0 * refined - norm_a2 - norm_b2 + offset
    weights = jnp.exp(refined - norm_b2).astype(jnp.bfloat16)
    transfer_terms = jnp.einsum(
        "xyuv,uvc->xyc", weights, rows_b, preferred_element_type=jnp.float32
    )
    warped = lax.psum_scatter(transfer_terms, "ba", scatter_dimension=1, tiled=True)
    return (log_mutual, warped)


def solution(mesh):
    placed = (P("aa", "ba", None), P("ba", "aa", None), P(), P(), P())
    return jax.shard_map(
        local,
        mesh=mesh,
        in_specs=placed,
        out_specs=(P("aa", None, "ba", None), P("aa", "ba", None)),
        check_vma=False,
    )
```

profile of v0, /device:TPU:0, one launch (start us, length us, event | category | flops | bytes accessed | tf_op | source)
XLA Modules:
  0.0 315.4 jit_solution(11921888077074273181)
XLA Ops:
  7.2 32.8 %all_gather.7 = bf16[4,128,256]{2,1,0:T(8,128)(2,1)S(1)} all-gather(bf16[4,16,256]{2,1,0:T(8,128)(2,1)} %param.6), channel_id=1, replica_groups=mesh['aa'=8,'ba'=4] {'aa'}, dimensions={1}, use_global_device_ids=true | all-gather | bytes 294912 | tf_op jit(solution)/shard_map/all_gather | solution.py:85
  40.0 5.4 %all_gather.6 = bf16[2,32,256]{2,1,0:T(8,128)(2,1)S(1)} all-gather(bf16[2,8,256]{2,1,0:T(8,128)(2,1)} %param.5), channel_id=1, replica_groups=mesh['aa'=8,'ba'=4] {'ba'}, dimensions={1}, use_global_device_ids=true | all-gather | bytes 40960 | tf_op jit(solution)/shard_map/all_gather | solution.py:84
  45.6 21.4 %pmax.28 = f32[4,128]{1,0:T(4,128)S(1)} all-reduce(f32[4,128]{1,0:T(4,128)S(1)} %get-tuple-element.348), channel_id=1, replica_groups=mesh['aa'=8,'ba'=4] {'aa'}, use_global_device_ids=true, to_apply=%region_1.0 | all-reduce | flops 512 | bytes 4096 | tf_op jit(solution)/shard_map/pmax | solution.py:73
  67.1 5.7 %pmax.29 = f32[2,32]{1,0:T(2,128)S(1)} all-reduce(f32[2,32]{1,0:T(2,128)S(1)} %get-tuple-element.92), channel_id=1, replica_groups=mesh['aa'=8,'ba'=4] {'ba'}, use_global_device_ids=true, to_apply=%region_5.0 | all-reduce | flops 64 | bytes 512 | tf_op jit(solution)/shard_map/pmax | solution.py:74
  72.9 6.6 %psum.29 = f32[2,32]{1,0:T(2,128)S(1)} all-reduce(f32[2,32]{1,0:T(2,128)S(1)} %exponential_reduce_fusion.2), channel_id=1, replica_groups=mesh['aa'=8,'ba'=4] {'ba'}, use_global_device_ids=true, to_apply=%region_7.0 | all-reduce | flops 64 | bytes 512 | tf_op jit(solution)/shard_map/psum | solution.py:76
  79.6 17.1 %psum.28 = f32[4,128]{1,0:T(4,128)S(1)} all-reduce(f32[4,128]{1,0:T(4,128)S(1)} %get-tuple-element.91), channel_id=1, replica_groups=mesh['aa'=8,'ba'=4] {'aa'}, use_global_device_ids=true, to_apply=%region_3.0 | all-reduce | flops 512 | bytes 4096 | tf_op jit(solution)/shard_map/psum | solution.py:75
  96.9 4.0 %collective-permute-start = (f32[1,32,4,128]{3,1,2,0:T(8,128)S(1)}, f32[1,32,4,128]{3,1,2,0:T(8,128)S(1)}, u32[]{:S(2)}, u32[]{:S(2)}) collective-permute-start(f32[1,32,4,128]{3,1,2,0:T(8,128)S(1)} %get-tuple-element.184), channel_id=1, source_target_pairs={{0,4},{4,8},{8,12},{12,16},{16,20},{20,24},{24,28},{1,5},{5,9},{9,... | collective-permute-start | bytes 196616 | tf_op jit(solution)/shard_map/ppermute | solution.py:16
  166.7 12.1 %add_maximum_fusion = f32[8,2,32,4,128]{4,0,3,2,1:T(8,128)S(1)} fusion(f32[8]{0:T(128)} %param.8, f32[2,32,4,128]{3,2,1,0:T(4,128)} %copy.169, f32[8]{0:T(128)} %get-tuple-element.346, f32[2,32,4,128]{3,2,1,0:T(4,128)} %copy.168, f32[8]{0:T(128)} %get-tuple-element.347, f32[2,32,4,128]{3,2,1,0:T(4,128)} %copy.167, f32[8]{0:T(128)S(1)} %get-tuple-element.268, ...), kind=kLoop, calls=%fused_computation.181 | loop fusion | flops 42729472 | bytes 11668032 | tf_op jit(solution)/shard_map/jit(relu)/max | solution.py:50
  178.9 4.6 %collective-permute-start.4 = (f32[8,1,32,4,128]{4,0,3,2,1:T(8,128)S(1)}, f32[8,1,32,4,128]{4,0,3,2,1:T(8,128)S(1)}, u32[]{:S(2)}, u32[]{:S(2)}) collective-permute-start(f32[8,1,32,4,128]{4,0,3,2,1:T(8,128)S(1)} %get-tuple-element.98), channel_id=1, source_target_pairs={{0,4},{4,8},{8,12},{12,16},{16,20},{20,24},{24,28},{1,5},{5,9},{9,... | collective-permute-start | bytes 1572872 | tf_op jit(solution)/shard_map/ppermute | solution.py:16
  187.4 17.6 %collective-permute-done.4 = f32[8,1,32,4,128]{4,0,3,2,1:T(8,128)S(1)} collective-permute-done((f32[8,1,32,4,128]{4,0,3,2,1:T(8,128)S(1)}, f32[8,1,32,4,128]{4,0,3,2,1:T(8,128)S(1)}, u32[]{:S(2)}, u32[]{:S(2)}) %collective-permute-start.4) | collective-permute-done | bytes 524320 | tf_op jit(solution)/shard_map/ppermute | solution.py:16
  205.1 4.0 %collective-permute-start.6 = (f32[8,4,32,1,128]{4,0,3,2,1:T(8,128)S(1)}, f32[8,4,32,1,128]{4,0,3,2,1:T(8,128)S(1)}, u32[]{:S(2)}, u32[]{:S(2)}) collective-permute-start(f32[8,4,32,1,128]{4,0,3,2,1:T(8,128)S(1)} %get-tuple-element.96), channel_id=1, source_target_pairs={{0,1},{1,2},{2,3},{4,5},{5,6},{6,7},{8,9},{9,10},{10,11},{12,13},{... | collective-permute-start | bytes 1572872 | tf_op jit(solution)/shard_map/ppermute | solution.py:16
  218.8 4.0 %select_maximum_fusion = f32[8,4,34,6,130]{4,0,3,2,1:T(8,128)S(1)} fusion(f32[8,4,32,1,128]{4,0,3,2,1:T(8,128)S(1)} %collective-permute-done.7, f32[8,4,32,1,128]{4,0,3,2,1:T(8,128)S(1)} %collective-permute-done.6, f32[8,1,32,4,128]{4,0,3,2,1:T(8,128)S(1)} %collective-permute-done.5, f32[8,2,32,4,128]{4,0,3,2,1:T(8,128)S(1)} %add_maximum_fusion, ...), kind=kLoop, calls=%fused_computation.4 | loop fusion | flops 17821440 | bytes 6540288 | tf_op jit(solution)/shard_map/concatenate | solution.py:14
  222.8 3.2 %fusion.81 = (f32[2,32,4,128]{3,2,1,0:T(4,128)S(1)}, f32[2,32,4,128]{3,2,1,0:T(4,128)S(1)}, f32[2,32,4,128]{3,2,1,0:T(4,128)S(1)}, f32[2,32,4,128]{3,2,1,0:T(4,1...) fusion(f32[8,4,34,6,130]{4,0,3,2,1:T(8,128)S(1)} %select_maximu, ...), kind=kLoop, calls=%fused_computation.173 | loop fusion | flops 4423680 | bytes 10617120 | tf_op jit(solution)/shard_map/reduce_sum | solution.py:64
  226.0 3.2 %fusion.80 = (f32[2,32,4,128]{3,2,1,0:T(4,128)S(1)}, f32[2,32,4,128]{3,2,1,0:T(4,128)S(1)}, f32[2,32,4,128]{3,2,1,0:T(4,128)S(1)}, f32[2,32,4,128]{3,2,1,0:T(4,1...) fusion(f32[8,4,34,6,130]{4,0,3,2,1:T(8,128)S(1)} %select_maximu, ...), kind=kLoop, calls=%fused_computation.171 | loop fusion | flops 4423680 | bytes 10617120 | tf_op jit(solution)/shard_map/reduce_sum | solution.py:64
  229.2 3.3 %fusion.79 = (f32[2,32,4,128]{3,2,1,0:T(4,128)S(1)}, f32[2,32,4,128]{3,2,1,0:T(4,128)S(1)}, f32[2,32,4,128]{3,2,1,0:T(4,128)S(1)}, f32[2,32,4,128]{3,2,1,0:T(4,1...) fusion(f32[8,4,34,6,130]{4,0,3,2,1:T(8,128)S(1)} %select_maximu, ...), kind=kLoop, calls=%fused_computation.169 | loop fusion | flops 4423680 | bytes 10617120 | tf_op jit(solution)/shard_map/reduce_sum | solution.py:64
  232.5 3.6 %fusion.78 = (f32[2,32,4,128]{3,2,1,0:T(4,128)S(1)}, f32[2,32,4,128]{3,2,1,0:T(4,128)S(1)}, f32[2,32,4,128]{3,2,1,0:T(4,128)S(1)}, f32[2,32,4,128]{3,2,1,0:T(4,1...) fusion(f32[8,4,34,6,130]{4,0,3,2,1:T(8,128)S(1)} %select_maximu, ...), kind=kLoop, calls=%fused_computation.167 | loop fusion | flops 4423680 | bytes 10617120 | tf_op jit(solution)/shard_map/reduce_sum | solution.py:64
  236.2 3.2 %fusion.83 = (f32[2,32,4,128]{3,2,1,0:T(4,128)S(1)}, f32[2,32,4,128]{3,2,1,0:T(4,128)S(1)}, f32[2,32,4,128]{3,2,1,0:T(4,128)S(1)}, f32[2,32,4,128]{3,2,1,0:T(4,1...) fusion(f32[8,4,34,6,130]{4,0,3,2,1:T(8,128)S(1)} %select_maximu, ...), kind=kLoop, calls=%fused_computation.177 | loop fusion | flops 4423680 | bytes 10617120 | tf_op jit(solution)/shard_map/reduce_sum | solution.py:64
  239.5 4.1 %fusion.82 = (f32[2,32,4,128]{3,2,1,0:T(4,128)}, f32[2,32,4,128]{3,2,1,0:T(4,128)}, f32[2,32,4,128]{3,2,1,0:T(4,128)}, f32[2,32,4,128]{3,2,1,0:T(4,128)}, f32[2,...) fusion(f32[8,4,34,6,130]{4,0,3,2,1:T(8,128)S(1)} %select_maximu, ...), kind=kLoop, calls=%fused_computation.175 | loop fusion | flops 4423680 | bytes 10617120 | tf_op jit(solution)/shard_map/reduce_sum | solution.py:64
  243.6 4.1 %fusion.84 = (f32[2,32,4,128]{3,2,1,0:T(4,128)}, f32[2,32,4,128]{3,2,1,0:T(4,128)}, f32[2,32,4,128]{3,2,1,0:T(4,128)}, f32[2,32,4,128]{3,2,1,0:T(4,128)}, f32[2,...) fusion(f32[8,4,34,6,130]{4,0,3,2,1:T(8,128)S(1)} %select_maximu, ...), kind=kLoop, calls=%fused_computation.179 | loop fusion | flops 4423680 | bytes 10617120 | tf_op jit(solution)/shard_map/reduce_sum | solution.py:64
  247.7 4.2 %fusion.77 = (f32[2,32,4,128]{3,2,1,0:T(4,128)}, f32[2,32,4,128]{3,2,1,0:T(4,128)}, f32[2,32,4,128]{3,2,1,0:T(4,128)}, f32[2,32,4,128]{3,2,1,0:T(4,128)}, f32[2,...) fusion(f32[8,4,34,6,130]{4,0,3,2,1:T(8,128)S(1)} %select_maximu, ...), kind=kLoop, calls=%fused_computation.165 | loop fusion | flops 4423680 | bytes 10617120 | tf_op jit(solution)/shard_map/reduce_sum | solution.py:64
  255.0 19.3 %pmax.30 = f32[4,128]{1,0:T(4,128)S(1)} all-reduce(f32[4,128]{1,0:T(4,128)S(1)} %get-tuple-element.89), channel_id=1, replica_groups=mesh['aa'=8,'ba'=4] {'aa'}, use_global_device_ids=true, to_apply=%region_90.91 | all-reduce | flops 512 | bytes 4096 | tf_op jit(solution)/shard_map/pmax | solution.py:73
  274.3 7.8 %pmax.31 = f32[2,32]{1,0:T(2,128)S(1)} all-reduce(f32[2,32]{1,0:T(2,128)S(1)} %get-tuple-element.90), channel_id=1, replica_groups=mesh['aa'=8,'ba'=4] {'ba'}, use_global_device_ids=true, to_apply=%region_94.95 | all-reduce | flops 64 | bytes 512 | tf_op jit(solution)/shard_map/pmax | solution.py:74
  282.3 7.2 %psum.31 = f32[2,32]{1,0:T(2,128)S(1)} all-reduce(f32[2,32]{1,0:T(2,128)S(1)} %get-tuple-element.88), channel_id=1, replica_groups=mesh['aa'=8,'ba'=4] {'ba'}, use_global_device_ids=true, to_apply=%region_96.97 | all-reduce | flops 64 | bytes 512 | tf_op jit(solution)/shard_map/psum | solution.py:76
  290.4 17.1 %psum.30 = f32[4,128]{1,0:T(4,128)S(1)} all-reduce(f32[4,128]{1,0:T(4,128)S(1)} %get-tuple-element.87), channel_id=1, replica_groups=mesh['aa'=8,'ba'=4] {'aa'}, use_global_device_ids=true, to_apply=%region_92.93 | all-reduce | flops 512 | bytes 4096 | tf_op jit(solution)/shard_map/psum | solution.py:75
  (159 shorter events, 85.1 us)
Async XLA Ops:
  7.2 301.2 %reduce-scatter.2.cloned.1.call-start = ((), (), s32[]{:S(2)}) async-start(), calls=%async_computation.1 | async-start | bytes 81920 | tf_op jit(solution)/shard_map/reduce_scatter | solution.py:109
  96.9 12.7 %collective-permute-start = (f32[1,32,4,128]{3,1,2,0:T(8,128)S(1)}, f32[1,32,4,128]{3,1,2,0:T(8,128)S(1)}, u32[]{:S(2)}, u32[]{:S(2)}) collective-permute-start(f32[1,32,4,128]{3,1,2,0:T(8,128)S(1)} %get-tuple-element.184), channel_id=1, source_target_pairs={{0,4},{4,8},{8,12},{12,16},{16,20},{20,24},{24,28},{1,5},{5,9},{9,... | collective-permute-start | bytes 196616 | tf_op jit(solution)/shard_map/ppermute | solution.py:16
  100.8 8.8 %collective-permute-start.1 = (f32[1,32,4,128]{3,1,2,0:T(8,128)S(1)}, f32[1,32,4,128]{3,1,2,0:T(8,128)S(1)}, u32[]{:S(2)}, u32[]{:S(2)}) collective-permute-start(f32[1,32,4,128]{3,1,2,0:T(8,128)S(1)} %get-tuple-element.185), channel_id=1, source_target_pairs={{4,0},{8,4},{12,8},{16,12},{20,16},{24,20},{28,24},{5,1},{9,5},{13... | collective-permute-start | bytes 196616 | tf_op jit(solution)/shard_map/ppermute | solution.py:18
  109.6 3.3 %collective-permute-start.2 = (f32[4,32,1,128]{3,1,2,0:T(8,128)S(1)}, f32[4,32,1,128]{3,1,2,0:T(8,128)S(1)}, u32[]{:S(2)}, u32[]{:S(2)}) collective-permute-start(f32[4,32,1,128]{3,1,2,0:T(8,128)S(1)} %get-tuple-element.180), channel_id=1, source_target_pairs={{0,1},{1,2},{2,3},{4,5},{5,6},{6,7},{8,9},{9,10},{10,11},{12,13},{... | collective-permute-start | bytes 196616 | tf_op jit(solution)/shard_map/ppermute | solution.py:16
  110.9 4.2 %collective-permute-start.3 = (f32[4,32,1,128]{3,1,2,0:T(8,128)S(1)}, f32[4,32,1,128]{3,1,2,0:T(8,128)S(1)}, u32[]{:S(2)}, u32[]{:S(2)}) collective-permute-start(f32[4,32,1,128]{3,1,2,0:T(8,128)S(1)} %get-tuple-element.181), channel_id=1, source_target_pairs={{1,0},{2,1},{3,2},{5,4},{6,5},{7,6},{9,8},{10,9},{11,10},{13,12},{... | collective-permute-start | bytes 196616 | tf_op jit(solution)/shard_map/ppermute | solution.py:18
  178.9 26.1 %collective-permute-start.4 = (f32[8,1,32,4,128]{4,0,3,2,1:T(8,128)S(1)}, f32[8,1,32,4,128]{4,0,3,2,1:T(8,128)S(1)}, u32[]{:S(2)}, u32[]{:S(2)}) collective-permute-start(f32[8,1,32,4,128]{4,0,3,2,1:T(8,128)S(1)} %get-tuple-element.98), channel_id=1, source_target_pairs={{0,4},{4,8},{8,12},{12,16},{16,20},{20,24},{24,28},{1,5},{5,9},{9,... | collective-permute-start | bytes 1572872 | tf_op jit(solution)/shard_map/ppermute | solution.py:16
  183.5 21.5 %collective-permute-start.5 = (f32[8,1,32,4,128]{4,0,3,2,1:T(8,128)S(1)}, f32[8,1,32,4,128]{4,0,3,2,1:T(8,128)S(1)}, u32[]{:S(2)}, u32[]{:S(2)}) collective-permute-start(f32[8,1,32,4,128]{4,0,3,2,1:T(8,128)S(1)} %get-tuple-element.99), channel_id=1, source_target_pairs={{4,0},{8,4},{12,8},{16,12},{20,16},{24,20},{28,24},{5,1},{9,5},{13... | collective-permute-start | bytes 1572872 | tf_op jit(solution)/shard_map/ppermute | solution.py:18
  205.1 9.9 %collective-permute-start.6 = (f32[8,4,32,1,128]{4,0,3,2,1:T(8,128)S(1)}, f32[8,4,32,1,128]{4,0,3,2,1:T(8,128)S(1)}, u32[]{:S(2)}, u32[]{:S(2)}) collective-permute-start(f32[8,4,32,1,128]{4,0,3,2,1:T(8,128)S(1)} %get-tuple-element.96), channel_id=1, source_target_pairs={{0,1},{1,2},{2,3},{4,5},{5,6},{6,7},{8,9},{9,10},{10,11},{12,13},{... | collective-permute-start | bytes 1572872 | tf_op jit(solution)/shard_map/ppermute | solution.py:16
  209.1 5.9 %collective-permute-start.7 = (f32[8,4,32,1,128]{4,0,3,2,1:T(8,128)S(1)}, f32[8,4,32,1,128]{4,0,3,2,1:T(8,128)S(1)}, u32[]{:S(2)}, u32[]{:S(2)}) collective-permute-start(f32[8,4,32,1,128]{4,0,3,2,1:T(8,128)S(1)} %get-tuple-element.97), channel_id=1, source_target_pairs={{1,0},{2,1},{3,2},{5,4},{6,5},{7,6},{9,8},{10,9},{11,10},{13,12},{... | collective-permute-start | bytes 1572872 | tf_op jit(solution)/shard_map/ppermute | solution.py:18
  232.5 3.7 %copy-start.3 = (f32[8]{0:T(128)S(1)}, f32[8]{0:T(128)}, u32[]{:S(2)}) copy-start(f32[8]{0:T(128)} %get-tuple-element.263) | copy-start | bytes 100
  236.1 3.4 %copy-start.2 = (f32[8]{0:T(128)S(1)}, f32[8]{0:T(128)}, u32[]{:S(2)}) copy-start(f32[8]{0:T(128)} %get-tuple-element.262) | copy-start | bytes 100
  236.1 3.4 %copy-start.4 = (f32[8]{0:T(128)S(1)}, f32[8]{0:T(128)}, u32[]{:S(2)}) copy-start(f32[8]{0:T(128)} %get-tuple-element.206) | copy-start | bytes 100
  236.1 3.4 %copy-start.5 = (f32[8]{0:T(128)S(1)}, f32[8]{0:T(128)}, u32[]{:S(2)}) copy-start(f32[8]{0:T(128)} %get-tuple-element.207) | copy-start | bytes 100
  236.1 3.4 %copy-start.6 = (f32[8]{0:T(128)S(1)}, f32[8]{0:T(128)}, u32[]{:S(2)}) copy-start(f32[8]{0:T(128)} %get-tuple-element.208) | copy-start | bytes 100
  236.1 3.4 %copy-start.7 = (f32[8]{0:T(128)S(1)}, f32[8]{0:T(128)}, u32[]{:S(2)}) copy-start(f32[8]{0:T(128)} %get-tuple-element.209) | copy-start | bytes 100
  236.1 3.4 %copy-start.8 = (f32[8]{0:T(128)S(1)}, f32[8]{0:T(128)}, u32[]{:S(2)}) copy-start(f32[8]{0:T(128)} %get-tuple-element.210) | copy-start | bytes 100
  236.1 3.4 %copy-start.9 = (f32[8]{0:T(128)S(1)}, f32[8]{0:T(128)}, u32[]{:S(2)}) copy-start(f32[8]{0:T(128)} %get-tuple-element.211) | copy-start | bytes 100
  236.1 3.4 %copy-start.10 = (f32[8]{0:T(128)S(1)}, f32[8]{0:T(128)}, u32[]{:S(2)}) copy-start(f32[8]{0:T(128)} %get-tuple-element.212) | copy-start | bytes 100
  236.1 3.4 %copy-start.11 = (f32[8]{0:T(128)S(1)}, f32[8]{0:T(128)}, u32[]{:S(2)}) copy-start(f32[8]{0:T(128)} %get-tuple-element.213) | copy-start | bytes 100
  239.4 4.2 %copy-start = (f32[8]{0:T(128)S(1)}, f32[8]{0:T(128)}, u32[]{:S(2)}) copy-start(f32[8]{0:T(128)} %get-tuple-element.264) | copy-start | bytes 100
  239.4 4.2 %copy-start.1 = (f32[8]{0:T(128)S(1)}, f32[8]{0:T(128)}, u32[]{:S(2)}) copy-start(f32[8]{0:T(128)} %get-tuple-element.266) | copy-start | bytes 100
Sparse Core Ops, SparseCore 0:
  290.5 16.0 reduce-scatter.1
where the time goes:
time: 319 us; the launch traced here: 315 us
  blocking collectives  140 us (44%)
  local copies, waits for them, and re-layouts  65 us (20%)
  other arithmetic  54.8 us (17%)
  waiting for transfers between devices  19.8 us (6%)
  starting transfers between devices  19.6 us (6%)
  between operations  14.8 us (5%)
    slice x85, local copies, waits for them, and re-layouts, spread_taps(): padded[offsets[0]:offsets[0] + extent[0], offsets[1]:offsets[1] + extent[...  51.2 us
    pmax x2, blocking collectives, dual_norms(): top_a = lax.pmax(jnp.max(values, axis=(0, 1)), 'aa')  40.7 us
    psum x2, blocking collectives, dual_norms(): mass_a = lax.psum(jnp.sum(jnp.exp(values - top_a), axis=(0, 1)), 'aa')  34.3 us
    reduce_sum x11, other arithmetic, reduce_taps(): jnp.sum(kernel[:, offsets[0], offsets[1], offsets[2], offsets[3]].reshape...  33.9 us
    all_gather x1, blocking collectives, local(): rows_b = lax.all_gather(features_b, 'aa', axis=1, tiled=True)  32.8 us
    ppermute x4, waiting for transfers between devices, padded_2(): lax.ppermute(tail, axis, [(i, (i + 1) % count) for i in range(ends)])  17.6 us
    psum x2, blocking collectives, dual_norms(): lax.psum(jnp.sum(jnp.exp(values - top_b[:, :, None, None]), axis=(2, 3)),...  13.9 us
    ppermute x4, starting transfers between devices, padded_2(): lax.ppermute(tail, axis, [(i, (i + 1) % count) for i in range(ends)])  13.8 us
  transfers between devices with their start and end apart: 9, of which 2 were waited for; matrix products, arithmetic and copies ran while one was open for 5% of the time, Pallas kernels for 0%

commit v1 on v0

--- a/solution.py
+++ b/solution.py
@@ -72,7 +72,7 @@
 def dual_norms(values):
     top_a = lax.pmax(jnp.max(values, axis=(0, 1)), "aa")
     top_b = lax.pmax(jnp.max(values, axis=(2, 3)), "ba")
-    mass_a = lax.psum(jnp.sum(jnp.exp(values - top_a), axis=(0, 1)), "aa")
+    mass_a = jnp.sum(lax.all_gather(jnp.sum(jnp.exp(values - top_a), axis=(0, 1)), "aa"), axis=0)
     mass_b = lax.psum(jnp.sum(jnp.exp(values - top_b[:, :, None, None]), axis=(2, 3)), "ba")
     norm_a = top_a + jnp.log(mass_a)
     norm_b = top_b + jnp.log(mass_b)

time: 319 us -> 335 us (1.050)
  blocking collectives: 140 us -> 160 us
    all_gather x0 -> x2, blocking collectives: none -> 52.2 us  [dual_norms(): lax.all_gather(jnp.sum(jnp.exp(values - top_a), axis=(0, 1)), 'aa')]
    psum x2 -> x0, blocking collectives: 34.3 us -> none  [dual_norms(): mass_a = lax.psum(jnp.sum(jnp.exp(values - top_a), axis=(0, 1)), 'aa')]
where the time goes in v1:
time: 335 us; the launch traced here: 332 us
  blocking collectives  160 us (48%)
  local copies, waits for them, and re-layouts  65 us (19%)
  other arithmetic  54.7 us (16%)
  waiting for transfers between devices  19.8 us (6%)
  starting transfers between devices  17.2 us (5%)
  between operations  14.8 us (4%)
    all_gather x2, blocking collectives, dual_norms(): lax.all_gather(jnp.sum(jnp.exp(values - top_a), axis=(0, 1)), 'aa')  52.2 us
    slice x85, local copies, waits for them, and re-layouts, spread_taps(): padded[offsets[0]:offsets[0] + extent[0], offsets[1]:offsets[1] + extent[...  51.2 us
    pmax x2, blocking collectives, dual_norms(): top_a = lax.pmax(jnp.max(values, axis=(0, 1)), 'aa')  41.8 us
    reduce_sum x11, other arithmetic, reduce_taps(): jnp.sum(kernel[:, offsets[0], offsets[1], offsets[2], offsets[3]].reshape...  33.9 us
    all_gather x1, blocking collectives, local(): rows_b = lax.all_gather(features_b, 'aa', axis=1, tiled=True)  32.8 us
    ppermute x4, waiting for transfers between devices, padded_2(): lax.ppermute(tail, axis, [(i, (i + 1) % count) for i in range(ends)])  17.6 us
    psum x2, blocking collectives, dual_norms(): lax.psum(jnp.sum(jnp.exp(values - top_b[:, :, None, None]), axis=(2, 3)),...  13.9 us
    pmax x2, blocking collectives, dual_norms(): top_b = lax.pmax(jnp.max(values, axis=(2, 3)), 'ba')  13.5 us
  transfers between devices with their start and end apart: 9, of which 2 were waited for; matrix products, arithmetic and copies ran while one was open for 5% of the time, Pallas kernels for 0%

profile of v1, /device:TPU:0, one launch (start us, length us, event | category | flops | bytes accessed | tf_op | source)
XLA Modules:
  0.0 332.2 jit_solution(8828996631137590380)
XLA Ops:
  7.2 32.8 %all_gather.19 = bf16[4,128,256]{2,1,0:T(8,128)(2,1)S(1)} all-gather(bf16[4,16,256]{2,1,0:T(8,128)(2,1)} %param.6), channel_id=1, replica_groups=mesh['aa'=8,'ba'=4] {'aa'}, dimensions={1}, use_global_device_ids=true | all-gather | bytes 294912 | tf_op jit(solution)/shard_map/all_gather | solution.py:85
  40.0 5.4 %all_gather.18 = bf16[2,32,256]{2,1,0:T(8,128)(2,1)S(1)} all-gather(bf16[2,8,256]{2,1,0:T(8,128)(2,1)} %param.5), channel_id=1, replica_groups=mesh['aa'=8,'ba'=4] {'ba'}, dimensions={1}, use_global_device_ids=true | all-gather | bytes 40960 | tf_op jit(solution)/shard_map/all_gather | solution.py:84
  45.6 21.4 %pmax.28 = f32[4,128]{1,0:T(4,128)S(1)} all-reduce(f32[4,128]{1,0:T(4,128)S(1)} %get-tuple-element.350), channel_id=1, replica_groups=mesh['aa'=8,'ba'=4] {'aa'}, use_global_device_ids=true, to_apply=%region_1.0 | all-reduce | flops 512 | bytes 4096 | tf_op jit(solution)/shard_map/pmax | solution.py:73
  67.1 5.7 %pmax.29 = f32[2,32]{1,0:T(2,128)S(1)} all-reduce(f32[2,32]{1,0:T(2,128)S(1)} %get-tuple-element.94), channel_id=1, replica_groups=mesh['aa'=8,'ba'=4] {'ba'}, use_global_device_ids=true, to_apply=%region_5.0 | all-reduce | flops 64 | bytes 512 | tf_op jit(solution)/shard_map/pmax | solution.py:74
  72.9 6.6 %psum.14 = f32[2,32]{1,0:T(2,128)S(1)} all-reduce(f32[2,32]{1,0:T(2,128)S(1)} %exponential_reduce_fusion.2), channel_id=1, replica_groups=mesh['aa'=8,'ba'=4] {'ba'}, use_global_device_ids=true, to_apply=%region_7.0 | all-reduce | flops 64 | bytes 512 | tf_op jit(solution)/shard_map/psum | solution.py:76
  79.5 26.1 %all-gather.2 = f32[8,4,128]{2,1,0:T(4,128)S(1)} all-gather(f32[1,4,128]{2,1,0:T(4,128)S(1)} %bitcast.344), channel_id=2, replica_groups=mesh['aa'=8,'ba'=4] {'aa'}, dimensions={0}, use_global_device_ids=true | all-gather | bytes 18432 | tf_op jit(solution)/shard_map/all_gather | solution.py:75
  173.1 12.0 %add_maximum_fusion = f32[8,2,32,4,128]{4,0,3,2,1:T(8,128)S(1)} fusion(f32[8]{0:T(128)} %param.8, f32[2,32,4,128]{3,2,1,0:T(4,128)} %copy.251, f32[8]{0:T(128)} %get-tuple-element.348, f32[2,32,4,128]{3,2,1,0:T(4,128)} %copy.250, f32[8]{0:T(128)} %get-tuple-element.349, f32[2,32,4,128]{3,2,1,0:T(4,128)} %copy.249, f32[8]{0:T(128)S(1)} %get-tuple-element.270, ...), kind=kLoop, calls=%fused_computation.181 | loop fusion | flops 42729472 | bytes 11668032 | tf_op jit(solution)/shard_map/jit(relu)/max | solution.py:50
  185.2 4.9 %collective-permute-start.4 = (f32[8,1,32,4,128]{4,0,3,2,1:T(8,128)S(1)}, f32[8,1,32,4,128]{4,0,3,2,1:T(8,128)S(1)}, u32[]{:S(2)}, u32[]{:S(2)}) collective-permute-start(f32[8,1,32,4,128]{4,0,3,2,1:T(8,128)S(1)} %get-tuple-element.100), channel_id=1, source_target_pairs={{0,4},{4,8},{8,12},{12,16},{16,20},{20,24},{24,28},{1,5},{5,9},{9,... | collective-permute-start | bytes 1572872 | tf_op jit(solution)/shard_map/ppermute | solution.py:16
  194.0 17.6 %collective-permute-done.4 = f32[8,1,32,4,128]{4,0,3,2,1:T(8,128)S(1)} collective-permute-done((f32[8,1,32,4,128]{4,0,3,2,1:T(8,128)S(1)}, f32[8,1,32,4,128]{4,0,3,2,1:T(8,128)S(1)}, u32[]{:S(2)}, u32[]{:S(2)}) %collective-permute-start.4) | collective-permute-done | bytes 524320 | tf_op jit(solution)/shard_map/ppermute | solution.py:16
  211.7 4.0 %collective-permute-start.6 = (f32[8,4,32,1,128]{4,0,3,2,1:T(8,128)S(1)}, f32[8,4,32,1,128]{4,0,3,2,1:T(8,128)S(1)}, u32[]{:S(2)}, u32[]{:S(2)}) collective-permute-start(f32[8,4,32,1,128]{4,0,3,2,1:T(8,128)S(1)} %get-tuple-element.98), channel_id=1, source_target_pairs={{0,1},{1,2},{2,3},{4,5},{5,6},{6,7},{8,9},{9,10},{10,11},{12,13},{... | collective-permute-start | bytes 1572872 | tf_op jit(solution)/shard_map/ppermute | solution.py:16
  225.4 4.0 %select_maximum_fusion = f32[8,4,34,6,130]{4,0,3,2,1:T(8,128)S(1)} fusion(f32[8,4,32,1,128]{4,0,3,2,1:T(8,128)S(1)} %collective-permute-done.7, f32[8,4,32,1,128]{4,0,3,2,1:T(8,128)S(1)} %collective-permute-done.6, f32[8,1,32,4,128]{4,0,3,2,1:T(8,128)S(1)} %collective-permute-done.5, f32[8,2,32,4,128]{4,0,3,2,1:T(8,128)S(1)} %add_maximum_fusion, ...), kind=kLoop, calls=%fused_computation.4 | loop fusion | flops 17821440 | bytes 6540288 | tf_op jit(solution)/shard_map/concatenate | solution.py:14
  229.4 3.2 fusion.81
  232.6 3.2 fusion.80
  235.8 3.3 fusion.79
  239.1 3.6 %fusion.78 = (f32[2,32,4,128]{3,2,1,0:T(4,128)S(1)}, f32[2,32,4,128]{3,2,1,0:T(4,128)S(1)}, f32[2,32,4,128]{3,2,1,0:T(4,128)S(1)}, f32[2,32,4,128]{3,2,1,0:T(4,1...) fusion(f32[8,4,34,6,130]{4,0,3,2,1:T(8,128)S(1)} %select_maximu, ...), kind=kLoop, calls=%fused_computation.167 | loop fusion | flops 4423680 | bytes 10617120 | tf_op jit(solution)/shard_map/reduce_sum | solution.py:64
  242.8 3.2 fusion.83
  246.1 4.1 %fusion.82 = (f32[2,32,4,128]{3,2,1,0:T(4,128)}, f32[2,32,4,128]{3,2,1,0:T(4,128)}, f32[2,32,4,128]{3,2,1,0:T(4,128)}, f32[2,32,4,128]{3,2,1,0:T(4,128)}, f32[2,...) fusion(f32[8,4,34,6,130]{4,0,3,2,1:T(8,128)S(1)} %select_maximu, ...), kind=kLoop, calls=%fused_computation.175 | loop fusion | flops 4423680 | bytes 10617120 | tf_op jit(solution)/shard_map/reduce_sum | solution.py:64
  250.2 4.1 %fusion.84 = (f32[2,32,4,128]{3,2,1,0:T(4,128)}, f32[2,32,4,128]{3,2,1,0:T(4,128)}, f32[2,32,4,128]{3,2,1,0:T(4,128)}, f32[2,32,4,128]{3,2,1,0:T(4,128)}, f32[2,...) fusion(f32[8,4,34,6,130]{4,0,3,2,1:T(8,128)S(1)} %select_maximu, ...), kind=kLoop, calls=%fused_computation.179 | loop fusion | flops 4423680 | bytes 10617120 | tf_op jit(solution)/shard_map/reduce_sum | solution.py:64
  254.3 4.2 %fusion.77 = (f32[2,32,4,128]{3,2,1,0:T(4,128)}, f32[2,32,4,128]{3,2,1,0:T(4,128)}, f32[2,32,4,128]{3,2,1,0:T(4,128)}, f32[2,32,4,128]{3,2,1,0:T(4,128)}, f32[2,...) fusion(f32[8,4,34,6,130]{4,0,3,2,1:T(8,128)S(1)} %select_maximu, ...), kind=kLoop, calls=%fused_computation.165 | loop fusion | flops 4423680 | bytes 10617120 | tf_op jit(solution)/shard_map/reduce_sum | solution.py:64
  258.5 3.1 fusion.95
  261.6 20.4 %pmax.30 = f32[4,128]{1,0:T(4,128)S(1)} all-reduce(f32[4,128]{1,0:T(4,128)S(1)} %get-tuple-element.91), channel_id=1, replica_groups=mesh['aa'=8,'ba'=4] {'aa'}, use_global_device_ids=true, to_apply=%region_90.91 | all-reduce | flops 512 | bytes 4096 | tf_op jit(solution)/shard_map/pmax | solution.py:73
  282.0 7.8 %pmax.31 = f32[2,32]{1,0:T(2,128)S(1)} all-reduce(f32[2,32]{1,0:T(2,128)S(1)} %get-tuple-element.92), channel_id=1, replica_groups=mesh['aa'=8,'ba'=4] {'ba'}, use_global_device_ids=true, to_apply=%region_94.95 | all-reduce | flops 64 | bytes 512 | tf_op jit(solution)/shard_map/pmax | solution.py:74
  290.0 7.2 %psum.15 = f32[2,32]{1,0:T(2,128)S(1)} all-reduce(f32[2,32]{1,0:T(2,128)S(1)} %get-tuple-element.90), channel_id=1, replica_groups=mesh['aa'=8,'ba'=4] {'ba'}, use_global_device_ids=true, to_apply=%region_96.97 | all-reduce | flops 64 | bytes 512 | tf_op jit(solution)/shard_map/psum | solution.py:76
  298.1 26.1 %all-gather.3 = f32[8,4,128]{2,1,0:T(4,128)S(1)} all-gather(f32[1,4,128]{2,1,0:T(4,128)S(1)} %bitcast.343), channel_id=3, replica_groups=mesh['aa'=8,'ba'=4] {'aa'}, dimensions={0}, use_global_device_ids=true | all-gather | bytes 18432 | tf_op jit(solution)/shard_map/all_gather | solution.py:75
  (161 shorter events, 83.4 us)
Async XLA Ops:
  7.2 318.0 %reduce-scatter.2.cloned.1.call-start = ((), (), s32[]{:S(2)}) async-start(), calls=%async_computation.1 | async-start | bytes 81920 | tf_op jit(solution)/shard_map/reduce_scatter | solution.py:109
  105.9 10.1 %collective-permute-start = (f32[1,32,4,128]{3,1,2,0:T(8,128)S(1)}, f32[1,32,4,128]{3,1,2,0:T(8,128)S(1)}, u32[]{:S(2)}, u32[]{:S(2)}) collective-permute-start(f32[1,32,4,128]{3,1,2,0:T(8,128)S(1)} %get-tuple-element.186), channel_id=1, source_target_pairs={{0,4},{4,8},{8,12},{12,16},{16,20},{20,24},{24,28},{1,5},{5,9},{9,... | collective-permute-start | bytes 196616 | tf_op jit(solution)/shard_map/ppermute | solution.py:16
  107.2 8.8 %collective-permute-start.1 = (f32[1,32,4,128]{3,1,2,0:T(8,128)S(1)}, f32[1,32,4,128]{3,1,2,0:T(8,128)S(1)}, u32[]{:S(2)}, u32[]{:S(2)}) collective-permute-start(f32[1,32,4,128]{3,1,2,0:T(8,128)S(1)} %get-tuple-element.187), channel_id=1, source_target_pairs={{4,0},{8,4},{12,8},{16,12},{20,16},{24,20},{28,24},{5,1},{9,5},{13... | collective-permute-start | bytes 196616 | tf_op jit(solution)/shard_map/ppermute | solution.py:18
  116.0 3.3 %collective-permute-start.2 = (f32[4,32,1,128]{3,1,2,0:T(8,128)S(1)}, f32[4,32,1,128]{3,1,2,0:T(8,128)S(1)}, u32[]{:S(2)}, u32[]{:S(2)}) collective-permute-start(f32[4,32,1,128]{3,1,2,0:T(8,128)S(1)} %get-tuple-element.182), channel_id=1, source_target_pairs={{0,1},{1,2},{2,3},{4,5},{5,6},{6,7},{8,9},{9,10},{10,11},{12,13},{... | collective-permute-start | bytes 196616 | tf_op jit(solution)/shard_map/ppermute | solution.py:16
  117.3 4.2 %collective-permute-start.3 = (f32[4,32,1,128]{3,1,2,0:T(8,128)S(1)}, f32[4,32,1,128]{3,1,2,0:T(8,128)S(1)}, u32[]{:S(2)}, u32[]{:S(2)}) collective-permute-start(f32[4,32,1,128]{3,1,2,0:T(8,128)S(1)} %get-tuple-element.183), channel_id=1, source_target_pairs={{1,0},{2,1},{3,2},{5,4},{6,5},{7,6},{9,8},{10,9},{11,10},{13,12},{... | collective-permute-start | bytes 196616 | tf_op jit(solution)/shard_map/ppermute | solution.py:18
  185.2 26.4 %collective-permute-start.4 = (f32[8,1,32,4,128]{4,0,3,2,1:T(8,128)S(1)}, f32[8,1,32,4,128]{4,0,3,2,1:T(8,128)S(1)}, u32[]{:S(2)}, u32[]{:S(2)}) collective-permute-start(f32[8,1,32,4,128]{4,0,3,2,1:T(8,128)S(1)} %get-tuple-element.100), channel_id=1, source_target_pairs={{0,4},{4,8},{8,12},{12,16},{16,20},{20,24},{24,28},{1,5},{5,9},{9,... | collective-permute-start | bytes 1572872 | tf_op jit(solution)/shard_map/ppermute | solution.py:16
  190.1 21.5 %collective-permute-start.5 = (f32[8,1,32,4,128]{4,0,3,2,1:T(8,128)S(1)}, f32[8,1,32,4,128]{4,0,3,2,1:T(8,128)S(1)}, u32[]{:S(2)}, u32[]{:S(2)}) collective-permute-start(f32[8,1,32,4,128]{4,0,3,2,1:T(8,128)S(1)} %get-tuple-element.101), channel_id=1, source_target_pairs={{4,0},{8,4},{12,8},{16,12},{20,16},{24,20},{28,24},{5,1},{9,5},{13... | collective-permute-start | bytes 1572872 | tf_op jit(solution)/shard_map/ppermute | solution.py:18
  211.7 9.9 %collective-permute-start.6 = (f32[8,4,32,1,128]{4,0,3,2,1:T(8,128)S(1)}, f32[8,4,32,1,128]{4,0,3,2,1:T(8,128)S(1)}, u32[]{:S(2)}, u32[]{:S(2)}) collective-permute-start(f32[8,4,32,1,128]{4,0,3,2,1:T(8,128)S(1)} %get-tuple-element.98), channel_id=1, source_target_pairs={{0,1},{1,2},{2,3},{4,5},{5,6},{6,7},{8,9},{9,10},{10,11},{12,13},{... | collective-permute-start | bytes 1572872 | tf_op jit(solution)/shard_map/ppermute | solution.py:16
  215.7 5.9 %collective-permute-start.7 = (f32[8,4,32,1,128]{4,0,3,2,1:T(8,128)S(1)}, f32[8,4,32,1,128]{4,0,3,2,1:T(8,128)S(1)}, u32[]{:S(2)}, u32[]{:S(2)}) collective-permute-start(f32[8,4,32,1,128]{4,0,3,2,1:T(8,128)S(1)} %get-tuple-element.99), channel_id=1, source_target_pairs={{1,0},{2,1},{3,2},{5,4},{6,5},{7,6},{9,8},{10,9},{11,10},{13,12},{... | collective-permute-start | bytes 1572872 | tf_op jit(solution)/shard_map/ppermute | solution.py:18
  239.1 3.7 %copy-start.3 = (f32[8]{0:T(128)S(1)}, f32[8]{0:T(128)}, u32[]{:S(2)}) copy-start(f32[8]{0:T(128)} %get-tuple-element.265) | copy-start | bytes 100
  242.7 3.4 %copy-start.2 = (f32[8]{0:T(128)S(1)}, f32[8]{0:T(128)}, u32[]{:S(2)}) copy-start(f32[8]{0:T(128)} %get-tuple-element.264) | copy-start | bytes 100
  242.7 3.4 %copy-start.4 = (f32[8]{0:T(128)S(1)}, f32[8]{0:T(128)}, u32[]{:S(2)}) copy-start(f32[8]{0:T(128)} %get-tuple-element.208) | copy-start | bytes 100
  242.7 3.4 %copy-start.5 = (f32[8]{0:T(128)S(1)}, f32[8]{0:T(128)}, u32[]{:S(2)}) copy-start(f32[8]{0:T(128)} %get-tuple-element.209) | copy-start | bytes 100
  242.7 3.4 %copy-start.6 = (f32[8]{0:T(128)S(1)}, f32[8]{0:T(128)}, u32[]{:S(2)}) copy-start(f32[8]{0:T(128)} %get-tuple-element.210) | copy-start | bytes 100
  242.7 3.4 %copy-start.7 = (f32[8]{0:T(128)S(1)}, f32[8]{0:T(128)}, u32[]{:S(2)}) copy-start(f32[8]{0:T(128)} %get-tuple-element.211) | copy-start | bytes 100
  242.7 3.4 %copy-start.8 = (f32[8]{0:T(128)S(1)}, f32[8]{0:T(128)}, u32[]{:S(2)}) copy-start(f32[8]{0:T(128)} %get-tuple-element.212) | copy-start | bytes 100
  242.7 3.4 %copy-start.9 = (f32[8]{0:T(128)S(1)}, f32[8]{0:T(128)}, u32[]{:S(2)}) copy-start(f32[8]{0:T(128)} %get-tuple-element.213) | copy-start | bytes 100
  242.7 3.4 %copy-start.10 = (f32[8]{0:T(128)S(1)}, f32[8]{0:T(128)}, u32[]{:S(2)}) copy-start(f32[8]{0:T(128)} %get-tuple-element.214) | copy-start | bytes 100
  242.8 3.4 %copy-start.11 = (f32[8]{0:T(128)S(1)}, f32[8]{0:T(128)}, u32[]{:S(2)}) copy-start(f32[8]{0:T(128)} %get-tuple-element.215) | copy-start | bytes 100
  246.0 4.2 %copy-start = (f32[8]{0:T(128)S(1)}, f32[8]{0:T(128)}, u32[]{:S(2)}) copy-start(f32[8]{0:T(128)} %get-tuple-element.266) | copy-start | bytes 100
  246.0 4.2 %copy-start.1 = (f32[8]{0:T(128)S(1)}, f32[8]{0:T(128)}, u32[]{:S(2)}) copy-start(f32[8]{0:T(128)} %get-tuple-element.268) | copy-start | bytes 100
Sparse Core Ops, SparseCore 0:
  298.3 16.0 reduce-scatter.1
